TPU v7x, 32 devices: a whole 2x2x4 slice. The times are simulated.
32 devices in a mesh: groups: 2 (over y), dap: 4 (over z), chan: 2 (over x), sub: 2 (over core).
Axes of the slice: x: 2, y: 2, z: 4, core: 2. Of those that a mesh axis runs over, the one named last changes fastest.
Arguments:
- pair_input: bfloat16 [768, 384, 128], P(('groups', 'dap'), ('chan', 'sub')), parts along dimension 0, may hold values from -6 to 6
- first_gain: float32 [128], replicated, may hold values from 0.25 to 1.75
- first_project: bfloat16 [128, 512], replicated, may hold values from -0.5 to 0.5
- first_gate: bfloat16 [128, 128], replicated, may hold values from -0.5 to 0.5
- first_norm: float32 [128], replicated, may hold values from 0.25 to 1.75
- first_final: bfloat16 [128, 128], replicated, may hold values from -0.5 to 0.5
- second_gain: float32 [128], replicated, may hold values from 0.25 to 1.75
- second_project: bfloat16 [128, 512], replicated, may hold values from -0.5 to 0.5
- second_gate: bfloat16 [128, 128], replicated, may hold values from -0.5 to 0.5
- second_norm: float32 [128], replicated, may hold values from 0.25 to 1.75
- second_final: bfloat16 [128, 128], replicated, may hold values from -0.5 to 0.5
Outputs:
- pair_output: bfloat16 [768, 384, 128], P(('groups', 'dap'), ('chan', 'sub')), parts along dimension 0
There are 2 independent parts, one for each index of `groups`. A program takes and returns all parts, laid end to end along the dimension named above; an argument that names none is the same for every part. Nothing has to cross between parts.
All inputs are finite; a program needn't handle non-finite values.
Results may differ from a plain program's by a relative error of at most 0.013.
Values may be sent and summed in bfloat16 or wider, within the bound.
No kernel may reach another device: no remote copies, remote signals or barrier semaphores. Data moves between devices by JAX's collectives and lax.ppermute only.
A program may use at most 64 MiB of HBM per device.

v0:
```python
import jax
import jax.numpy as jnp
from jax import lax
from jax.sharding import PartitionSpec as P

epsilon = 1e-05


def layer_norm(values, norm_gain, reduce_axis):
    average = jnp.mean(values, axis=reduce_axis, keepdims=True)
    centred = values - average
    variance = jnp.mean(centred * centred, axis=reduce_axis, keepdims=True)
    return centred * lax.rsqrt(variance + epsilon) * norm_gain


def project_in(pair_state, norm_gain, project, gate_matrix):
    row_count, col_count, features = pair_state.shape
    flattened = pair_state.reshape(row_count * col_count, features).astype(jnp.float32)
    normed = layer_norm(flattened, norm_gain, 1).astype(jnp.bfloat16)
    projected = jnp.einsum("xc,cd->dx", normed, project, preferred_element_type=jnp.float32)
    left_part = jax.nn.sigmoid(projected[:features]) * projected[features : 2 * features]
    right_part = jax.nn.sigmoid(projected[2 * features : 3 * features]) * projected[3 * features :]
    left_part = left_part.astype(jnp.bfloat16).reshape(features, row_count, col_count)
    right_part = right_part.astype(jnp.bfloat16).reshape(features, row_count, col_count)
    gating = jax.nn.sigmoid(jnp.dot(normed, gate_matrix, preferred_element_type=jnp.float32))
    return (left_part, right_part, gating)


def finish(pair_state, mixture, gating, out_gain, final_matrix):
    features = mixture.shape[0]
    flattened = mixture.reshape(features, -1).astype(jnp.float32)
    normed = layer_norm(flattened, out_gain[:, None], 0).astype(jnp.bfloat16)
    update = jnp.einsum("cx,cd->xd", normed, final_matrix, preferred_element_type=jnp.float32)
    result = pair_state.reshape(-1, features).astype(jnp.float32) + gating * update
    return result.astype(jnp.bfloat16).reshape(pair_state.shape)


def shards(
    pair_input,
    first_gain,
    first_project,
    first_gate,
    first_norm,
    first_final,
    second_gain,
    second_project,
    second_gate,
    second_norm,
    second_final,
):
    left_part, right_part, gating = project_in(pair_input, first_gain, first_project, first_gate)
    left_part, right_part = (
        lax.all_to_all(left_part, ("chan", "sub"), split_axis=0, concat_axis=2, tiled=True),
        lax.all_to_all(right_part, ("chan", "sub"), split_axis=0, concat_axis=2, tiled=True),
    )
    mixture = jnp.einsum(
        "cik,cjk->cij",
        left_part,
        lax.all_gather(right_part, "dap", axis=1, tiled=True),
        preferred_element_type=jnp.float32,
    ).astype(jnp.bfloat16)
    mixture = lax.all_to_all(mixture, ("chan", "sub"), split_axis=2, concat_axis=0, tiled=True)
    middle = finish(pair_input, mixture, gating, first_norm, first_final)
    left_part, right_part, gating = project_in(middle, second_gain, second_project, second_gate)
    left_part, right_part = (
        lax.all_to_all(left_part, ("chan", "sub"), split_axis=0, concat_axis=2, tiled=True),
        lax.all_to_all(right_part, ("chan", "sub"), split_axis=0, concat_axis=2, tiled=True),
    )
    turned = lax.all_to_all(left_part, "dap", split_axis=2, concat_axis=1, tiled=True)
    mixture = jnp.einsum(
        "cki,ckj->cij",
        turned,
        lax.all_gather(right_part, "dap", axis=1, tiled=True),
        preferred_element_type=jnp.float32,
    )
    mixture = lax.all_to_all(
        mixture.astype(jnp.bfloat16), ("chan", "sub"), split_axis=2, concat_axis=0, tiled=True
    )
    return finish(middle, mixture, gating, second_norm, second_final)


def solution(mesh):
    placed = (
        P(("groups", "dap"), ("chan", "sub"), None),
        P(),
        P(),
        P(),
        P(),
        P(),
        P(),
        P(),
        P(),
        P(),
        P(),
    )
    return jax.shard_map(
        shards,
        mesh=mesh,
        in_specs=placed,
        out_specs=P(("groups", "dap"), ("chan", "sub"), None),
        check_vma=False,
    )
```

profile of v0, /device:TPU:0, one launch (start us, length us, event | category | flops | bytes accessed | tf_op | source)
XLA Modules:
  0.0 717.1 jit_solution(18188985698345366559)
XLA Ops:
  31.6 41.2 %all_to_all.108 = bf16[128,96,96]{2,1,0:T(8,128)(2,1)S(1)} all-to-all(bf16[128,96,96]{2,1,0:T(8,128)(2,1)} %copy.28), channel_id=1, replica_groups=mesh['groups'=2,'dap'=4,'chan'=2,'sub'=2] {'chan','sub'}, dimensions={0} | all-to-all | bytes 4718592 | tf_op jit(solution)/shard_map/all_to_all | solution.py:54
  76.9 5.9 all_to_all.86
  87.7 53.0 %all_to_all.109 = bf16[128,96,96]{2,1,0:T(8,128)(2,1)S(1)} all-to-all(bf16[128,96,96]{2,1,0:T(8,128)(2,1)} %copy.26), channel_id=1, replica_groups=mesh['groups'=2,'dap'=4,'chan'=2,'sub'=2] {'chan','sub'}, dimensions={0} | all-to-all | bytes 4718592 | tf_op jit(solution)/shard_map/all_to_all | solution.py:53
  144.7 5.9 all_to_all.82
  150.7 100.2 %all-gather.3.cloned.1.call-done = bf16[32,384,384]{2,1,0:T(8,128)(2,1)} async-done(((bf16[32,96,384]{2,1,0:T(8,128)(2,1)}), bf16[32,384,384]{2,1,0:T(8,128)(2,1)}) %all-gather.3.cloned.1.call-update) | async-done | bytes 9437200 | tf_op jit(solution)/shard_map/all_gather | solution.py:59
  250.9 9.1 %convolution_convert_fusion.1 = bf16[32,96,384]{2,1,0:T(8,128)(2,1)} fusion(bf16[32,96,384]{2,1,0:T(8,128)(2,1)} %all_to_all.82, bf16[32,384,384]{2,1,0:T(8,128)(2,1)} %all-gather.3.cloned.1.call-done), kind=kOutput, calls=%fused_computation.61 | convolution fusion | flops 907149312 | bytes 14155776 | tf_op jit(solution)/shard_map/cik,cjk->cij/dot_general | solution.py:56
  269.7 5.2 fusion.9
  274.9 31.7 %all-to-all-done.2 = bf16[32,96,384]{1,0,2:T(8,128)(2,1)} async-done(((bf16[32,96,384]{1,0,2:T(8,128)(2,1)}), bf16[32,96,384]{1,0,2:T(8,128)(2,1)}, u32[]{:S(2)}, u32[]{:S(2)}) %all-to-all-start.2) | async-done | bytes 2359328 | tf_op jit(solution)/shard_map/all_to_all | solution.py:62
  306.6 6.9 copy.31
  319.2 7.2 %reshape.153 = f32[128,9216]{1,0:T(8,128)} reshape(f32[4,32,96,96]{3,2,1,0:T(8,128)} %bitcast.64) | data formatting | bytes 9437184 | tf_op jit(solution)/shard_map/convert_element_type | solution.py:31
  326.4 5.9 fusion.36
  346.1 40.8 %all_to_all.110 = bf16[128,96,96]{2,1,0:T(8,128)(2,1)S(1)} all-to-all(bf16[128,96,96]{2,1,0:T(8,128)(2,1)} %copy.37), channel_id=1, replica_groups=mesh['groups'=2,'dap'=4,'chan'=2,'sub'=2] {'chan','sub'}, dimensions={0} | all-to-all | bytes 4718592 | tf_op jit(solution)/shard_map/all_to_all | solution.py:67
  390.9 5.9 all_to_all.99
  400.1 42.3 %all_to_all.111 = bf16[128,96,96]{2,1,0:T(8,128)(2,1)} all-to-all(bf16[128,96,96]{2,1,0:T(8,128)(2,1)} %copy.32), channel_id=1, replica_groups=mesh['groups'=2,'dap'=4,'chan'=2,'sub'=2] {'chan','sub'}, dimensions={0} | all-to-all | bytes 4718592 | tf_op jit(solution)/shard_map/all_to_all | solution.py:66
  442.4 6.6 copy.41
  449.0 159.6 %all_to_all.112 = bf16[32,96,384]{1,0,2:T(8,128)(2,1)S(1)} all-to-all(bf16[32,96,384]{1,0,2:T(8,128)(2,1)} %bitcast.71), channel_id=1, replica_groups=mesh['groups'=2,'dap'=4,'chan'=2,'sub'=2] {'dap'}, dimensions={2} | all-to-all | bytes 4718592 | tf_op jit(solution)/shard_map/all_to_all | solution.py:69
  617.6 10.6 %all-gather.5.cloned.1.call-done = bf16[32,384,384]{2,1,0:T(8,128)(2,1)} async-done(((bf16[32,96,384]{2,1,0:T(8,128)(2,1)}), bf16[32,384,384]{2,1,0:T(8,128)(2,1)}) %all-gather.5.cloned.1.call-update) | async-done | bytes 9437200 | tf_op jit(solution)/shard_map/all_gather | solution.py:73
  628.2 7.0 convolution_convert_fusion
  635.2 5.0 copy.39
  645.1 6.7 fusion.10
  651.8 30.3 %all-to-all-done.6 = bf16[32,96,384]{1,0,2:T(8,128)(2,1)} async-done(((bf16[32,96,384]{1,0,2:T(8,128)(2,1)}), bf16[32,96,384]{1,0,2:T(8,128)(2,1)}, u32[]{:S(2)}, u32[]{:S(2)}) %all-to-all-start.6) | async-done | bytes 2359328 | tf_op jit(solution)/shard_map/all_to_all | solution.py:76
  682.1 6.9 copy.40
  694.7 7.2 %reshape.154 = f32[128,9216]{1,0:T(8,128)} reshape(f32[4,32,96,96]{3,2,1,0:T(8,128)} %bitcast.65) | data formatting | bytes 9437184 | tf_op jit(solution)/shard_map/convert_element_type | solution.py:31
  701.9 8.0 %fusion.7 = bf16[9216,128]{1,0:T(8,128)(2,1)} fusion(f32[9216,128]{1,0:T(8,128)} %copy-done.4, f32[9216,128]{1,0:T(8,128)} %fusion.10, bf16[128,128]{1,0:T(8,128)(2,1)S(1)} %copy-done.9, f32[128,9216]{1,0:T(8,128)} %reshape.154, f32[128]{0:T(128)S(1)} %copy-done.13, f32[9216]{0:T(1024)S(1)} %rsqrt.47, f32[9216]{0:T(1024)S(1)} %div.63), kind=kOutput, calls=%fused_computation.13 | convolution fusion | flops 310247424 | bytes 16622080 | tf_op jit(solution)/shard_map/cx,cd->xd/dot_general | solution.py:33
  (74 shorter events, 93.8 us)
Async XLA Ops:
  6.5 13.7 %copy-start = (bf16[128,512]{1,0:T(8,128)(2,1)S(1)}, bf16[128,512]{1,0:T(8,128)(2,1)}, u32[]{:S(2)}) copy-start(bf16[128,512]{1,0:T(8,128)(2,1)} %param.13) | copy-start | bytes 393220
  6.5 7.3 %copy-start.5 = (bf16[96,96,128]{2,1,0:T(8,128)(2,1)S(1)}, bf16[96,96,128]{2,1,0:T(8,128)(2,1)}, u32[]{:S(2)}) copy-start(bf16[96,96,128]{2,1,0:T(8,128)(2,1)} %param.11) | copy-start | bytes 7077892
  6.5 7.3 %copy-start.12 = (f32[128]{0:T(128)S(1)}, f32[128]{0:T(128)}, u32[]{:S(2)}) copy-start(f32[128]{0:T(128)} %param.12) | copy-start | bytes 1540
  6.5 244.4 %all-gather.3.cloned.1.call-start = ((), (), s32[]{:S(2)}) async-start(), calls=%async_computation.7 | async-start | bytes 11796480 | tf_op jit(solution)/shard_map/all_gather | solution.py:59
  18.9 1.4 copy-start.6
  260.0 9.7 %copy-start.14 = (bf16[128,128]{1,0:T(8,128)(2,1)S(1)}, bf16[128,128]{1,0:T(8,128)(2,1)}, u32[]{:S(2)}) copy-start(bf16[128,128]{1,0:T(8,128)(2,1)} %param.14) | copy-start | bytes 98308
  265.0 41.6 %all-to-all-start.2 = ((bf16[32,96,384]{1,0,2:T(8,128)(2,1)}), bf16[32,96,384]{1,0,2:T(8,128)(2,1)}, u32[]{:S(2)}, u32[]{:S(2)}) async-start(bf16[32,96,384]{1,0,2:T(8,128)(2,1)} %copy.30), calls=%async_computation.2 | async-start | bytes 6291456 | tf_op jit(solution)/shard_map/all_to_all | solution.py:62
  269.7 358.5 %all-gather.5.cloned.1.call-start = ((), (), s32[]{:S(2)}) async-start(), calls=%async_computation.8 | async-start | bytes 11796480 | tf_op jit(solution)/shard_map/all_gather | solution.py:73
  313.5 4.6 copy-start.2
  319.2 7.2 %copy-start.8 = (bf16[128,128]{1,0:T(8,128)(2,1)S(1)}, bf16[128,128]{1,0:T(8,128)(2,1)}, u32[]{:S(2)}) copy-start(bf16[128,128]{1,0:T(8,128)(2,1)} %param.16) | copy-start | bytes 98308
  319.2 7.2 %copy-start.11 = (f32[128]{0:T(128)S(1)}, f32[128]{0:T(128)}, u32[]{:S(2)}) copy-start(f32[128]{0:T(128)} %param.15) | copy-start | bytes 1540
  332.3 5.5 copy-start.4
  332.4 2.8 copy-start.7
  332.4 2.8 copy-start.10
  635.2 9.9 %copy-start.15 = (bf16[128,128]{1,0:T(8,128)(2,1)S(1)}, bf16[128,128]{1,0:T(8,128)(2,1)}, u32[]{:S(2)}) copy-start(bf16[128,128]{1,0:T(8,128)(2,1)} %param.19) | copy-start | bytes 98308
  640.2 41.8 %all-to-all-start.6 = ((bf16[32,96,384]{1,0,2:T(8,128)(2,1)}), bf16[32,96,384]{1,0,2:T(8,128)(2,1)}, u32[]{:S(2)}, u32[]{:S(2)}) async-start(bf16[32,96,384]{1,0,2:T(8,128)(2,1)} %copy.39), calls=%async_computation.6 | async-start | bytes 6291456 | tf_op jit(solution)/shard_map/all_to_all | solution.py:76
  689.0 4.6 copy-start.3
  694.6 7.2 %copy-start.9 = (bf16[128,128]{1,0:T(8,128)(2,1)S(1)}, bf16[128,128]{1,0:T(8,128)(2,1)}, u32[]{:S(2)}) copy-start(bf16[128,128]{1,0:T(8,128)(2,1)} %param.21) | copy-start | bytes 98308
  694.7 7.2 %copy-start.13 = (f32[128]{0:T(128)S(1)}, f32[128]{0:T(128)}, u32[]{:S(2)}) copy-start(f32[128]{0:T(128)} %param.20) | copy-start | bytes 1540
  694.7 15.2 %copy-start.1 = (bf16[128,512]{1,0:T(8,128)(2,1)S(1)}, bf16[128,512]{1,0:T(8,128)(2,1)}, u32[]{:S(2)}) copy-start(bf16[128,512]{1,0:T(8,128)(2,1)} %param.13) | copy-start | bytes 393220
Sparse Core Ops, SparseCore 0:
  83.0 167.8 all-gather.2
  397.0 231.1 all-gather.4
where the time goes:
time: 727 us; the launch traced here: 717 us
  blocking collectives  337 us (46%)
  waiting for transfers between devices  173 us (24%)
  local copies, waits for them, and re-layouts  106 us (15%)
  matrix products  47 us (6%)
  other arithmetic  30.8 us (4%)
  between operations  14.1 us (2%)
  starting transfers between devices  9.58 us (1%)
    all_to_all x1, blocking collectives, shards(): lax.all_to_all(left_part, 'dap', split_axis=2, concat_axis=1, tiled=True)  160 us
    all_gather x2, waiting for transfers between devices, shards(): lax.all_gather(right_part, 'dap', axis=1, tiled=True)  111 us
    all_to_all x2, blocking collectives, shards(): lax.all_to_all(left_part, ('chan', 'sub'), split_axis=0, concat_axis=2, t...  95.4 us
    all_to_all x2, blocking collectives, shards(): lax.all_to_all(right_part, ('chan', 'sub'), split_axis=0, concat_axis=2,...  82 us
    all_to_all x1, waiting for transfers between devices, shards(): lax.all_to_all(mixture, ('chan', 'sub'), split_axis=2, concat_axis=0, til...  31.7 us
    all_to_all x1, waiting for transfers between devices, shards(): lax.all_to_all(mixture.astype(jnp.bfloat16), ('chan', 'sub'), split_axis=...  30.3 us
    convert_element_type x4, local copies, waits for them, and re-layouts, finish(): flattened = mixture.reshape(features, -1).astype(jnp.float32)  28.1 us
    all_to_all x4, local copies, waits for them, and re-layouts, shards(): lax.all_to_all(right_part, ('chan', 'sub'), split_axis=0, concat_axis=2,...  20 us
  transfers between devices with their start and end apart: 4, of which 4 were waited for; matrix products, arithmetic and copies ran while one was open for 5% of the time, Pallas kernels for 0%

commit v1 on v0

--- a/solution.py
+++ b/solution.py
@@ -4,6 +4,20 @@
 from jax.sharding import PartitionSpec as P
 
 epsilon = 1e-05
+
+
+def on_each_block(array, axis, dim, make, out_dim):
+    ways, here, step = (lax.axis_size(axis), lax.axis_index(axis), array.shape[dim])
+    earlier, later = ([], [])
+    going_up = going_down = array
+    for far in range(ways // 2 + 1):
+        earlier.append(make(going_up, (here - far) % ways * step))
+        if 0 < far < ways - ways // 2:
+            later.append(make(going_down, (here + far) % ways * step))
+        going_up = lax.ppermute(going_up, axis, [(d, (d + 1) % ways) for d in range(ways)])
+        going_down = lax.ppermute(going_down, axis, [(d, (d - 1) % ways) for d in range(ways)])
+    line = jnp.concatenate([*earlier[::-1], *later], axis=out_dim)
+    return jnp.roll(line, (here - ways // 2) * earlier[0].shape[out_dim], axis=out_dim)
 
 
 def layer_norm(values, norm_gain, reduce_axis):
@@ -53,11 +67,14 @@
         lax.all_to_all(left_part, ("chan", "sub"), split_axis=0, concat_axis=2, tiled=True),
         lax.all_to_all(right_part, ("chan", "sub"), split_axis=0, concat_axis=2, tiled=True),
     )
-    mixture = jnp.einsum(
-        "cik,cjk->cij",
-        left_part,
-        lax.all_gather(right_part, "dap", axis=1, tiled=True),
-        preferred_element_type=jnp.float32,
+    mixture = on_each_block(
+        right_part,
+        "dap",
+        1,
+        lambda part, at: jnp.einsum(
+            "cik,cjk->cij", left_part, part, preferred_element_type=jnp.float32
+        ),
+        2,
     ).astype(jnp.bfloat16)
     mixture = lax.all_to_all(mixture, ("chan", "sub"), split_axis=2, concat_axis=0, tiled=True)
     middle = finish(pair_input, mixture, gating, first_norm, first_final)

time: 727 us -> 703 us (0.967)
  blocking collectives: 337 us -> 281 us
  waiting for transfers between devices: 173 us -> 199 us
    ppermute x0 -> x3, waiting for transfers between devices: none -> 124 us  [the longest x2 89.6 us: on_each_block(): lax.ppermute(going_up, axis, [(d, (d + 1) % ways) for d in range(ways)])]
    all_gather x2 -> x1, waiting for transfers between devices: 111 us -> 13 us  [shards(): lax.all_gather(right_part, 'dap', axis=1, tiled=True)]
    all_to_all x2 -> x1, blocking collectives: 95.4 us -> 40.7 us  [shards(): lax.all_to_all(left_part, ('chan', 'sub'), split_axis=0, concat_axis=2, t...]
    concatenate x0 -> x1, local copies, waits for them, and re-layouts: none -> 9.59 us  [on_each_block(): jnp.roll(line, (here - ways // 2) * earlier[0].shape[out_dim], axis=out_dim)]
    all_to_all x4, local copies, waits for them, and re-layouts: 20 us -> 11.3 us  [shards(): lax.all_to_all(right_part, ('chan', 'sub'), split_axis=0, concat_axis=2,...]
  transfers between devices with their start and end apart: 4 -> 7, of which waited for: 4 -> 6; matrix products, arithmetic and copies ran while one was open for 5% -> 6% of each run, Pallas kernels for 0% -> 0%
where the time goes in v1:
time: 703 us; the launch traced here: 693 us
  blocking collectives  281 us (40%)
  waiting for transfers between devices  199 us (28%)
  local copies, waits for them, and re-layouts  101 us (14%)
  matrix products  51.3 us (7%)
  other arithmetic  31.2 us (4%)
  starting transfers between devices  15.9 us (2%)
  between operations  14.2 us (2%)
    all_to_all x1, blocking collectives, shards(): lax.all_to_all(left_part, 'dap', split_axis=2, concat_axis=1, tiled=True)  160 us
    ppermute x2, waiting for transfers between devices, on_each_block(): lax.ppermute(going_up, axis, [(d, (d + 1) % ways) for d in range(ways)])  89.6 us
    all_to_all x2, blocking collectives, shards(): lax.all_to_all(right_part, ('chan', 'sub'), split_axis=0, concat_axis=2,...  80.6 us
    all_to_all x1, blocking collectives, shards(): lax.all_to_all(left_part, ('chan', 'sub'), split_axis=0, concat_axis=2, t...  40.7 us
    ppermute x1, waiting for transfers between devices, on_each_block(): lax.ppermute(going_down, axis, [(d, (d - 1) % ways) for d in range(ways)])  34.7 us
    all_to_all x1, waiting for transfers between devices, shards(): lax.all_to_all(mixture, ('chan', 'sub'), split_axis=2, concat_axis=0, til...  31.4 us
    all_to_all x1, waiting for transfers between devices, shards(): lax.all_to_all(mixture.astype(jnp.bfloat16), ('chan', 'sub'), split_axis=...  30.2 us
    convert_element_type x4, local copies, waits for them, and re-layouts, finish(): flattened = mixture.reshape(features, -1).astype(jnp.float32)  24.2 us
  transfers between devices with their start and end apart: 7, of which 6 were waited for; matrix products, arithmetic and copies ran while one was open for 6% of the time, Pallas kernels for 0%

profile of v1, /device:TPU:0, one launch (start us, length us, event | category | flops | bytes accessed | tf_op | source)
XLA Modules:
  0.0 693.4 jit_solution(16365149354332728784)
XLA Ops:
  13.9 4.9 fusion.29
  30.3 40.9 %all_to_all.108 = bf16[128,96,96]{2,1,0:T(8,128)(2,1)S(1)} all-to-all(bf16[128,96,96]{2,1,0:T(8,128)(2,1)S(1)} %copy.28), channel_id=1, replica_groups=mesh['groups'=2,'dap'=4,'chan'=2,'sub'=2] {'chan','sub'}, dimensions={0} | all-to-all | bytes 4718592 | tf_op jit(solution)/shard_map/all_to_all | solution.py:68
  89.2 43.9 %collective-permute-done = bf16[32,96,384]{2,1,0:T(8,128)(2,1)} collective-permute-done((bf16[32,96,384]{2,1,0:T(8,128)(2,1)}, bf16[32,96,384]{2,1,0:T(8,128)(2,1)}, u32[]{:S(2)}, u32[]{:S(2)}) %collective-permute-start) | collective-permute-done | bytes 2359328 | tf_op jit(solution)/shard_map/ppermute | solution.py:17
  137.8 5.0 all_to_all.82
  149.0 34.7 %collective-permute-done.2 = bf16[32,96,384]{2,1,0:T(8,128)(2,1)} collective-permute-done((bf16[32,96,384]{2,1,0:T(8,128)(2,1)}, bf16[32,96,384]{2,1,0:T(8,128)(2,1)}, u32[]{:S(2)}, u32[]{:S(2)}) %collective-permute-start.2) | collective-permute-done | bytes 2359328 | tf_op jit(solution)/shard_map/ppermute | solution.py:18
  187.2 45.7 %collective-permute-done.1 = bf16[32,96,384]{2,1,0:T(8,128)(2,1)} collective-permute-done((bf16[32,96,384]{2,1,0:T(8,128)(2,1)}, bf16[32,96,384]{2,1,0:T(8,128)(2,1)}, u32[]{:S(2)}, u32[]{:S(2)}) %collective-permute-start.1) | collective-permute-done | bytes 2359328 | tf_op jit(solution)/shard_map/ppermute | solution.py:17
  236.4 9.6 %concatenate.6 = bf16[32,96,768]{2,1,0:T(8,128)(2,1)} concatenate(bf16[32,96,96]{2,1,0:T(8,128)(2,1)} %fusion.37, bf16[32,96,96]{2,1,0:T(8,128)(2,1)} %fusion.38, bf16[32,96,96]{2,1,0:T(8,128)(2,1)S(1)} %fusion.39, bf16[32,96,96]{2,1,0:T(8,128)(2,1)} %fusion.40, bf16[32,96,96]{2,1,0:T(8,128)(2,1)} %fusion.37, bf16[32,96,96]{2,1,0:T(8,128)(2,1)} %fusion.38, ...), dimensions={2} | concatenate | bytes 9437184 | tf_op jit(solution)/shard_map/jit(_roll_dynamic)/concatenate | solution.py:20
  256.6 5.2 fusion.9
  261.8 31.4 %all-to-all-done.2 = bf16[32,96,384]{1,0,2:T(8,128)(2,1)S(1)} async-done(((bf16[32,96,384]{1,0,2:T(8,128)(2,1)}), bf16[32,96,384]{1,0,2:T(8,128)(2,1)S(1)}, u32[]{:S(2)}, u32[]{:S(2)}) %all-to-all-start.2) | async-done | bytes 2359328 | tf_op jit(solution)/shard_map/all_to_all | solution.py:79
  293.2 4.8 copy.31
  303.7 7.4 %reshape.153 = f32[128,9216]{1,0:T(8,128)} reshape(f32[4,32,96,96]{3,2,1,0:T(8,128)} %bitcast.70) | data formatting | bytes 9437184 | tf_op jit(solution)/shard_map/convert_element_type | solution.py:45
  311.1 5.9 fusion.36
  330.0 39.6 %all_to_all.109 = bf16[128,96,96]{2,1,0:T(8,128)(2,1)S(1)} all-to-all(bf16[128,96,96]{2,1,0:T(8,128)(2,1)S(1)} %copy.37), channel_id=1, replica_groups=mesh['groups'=2,'dap'=4,'chan'=2,'sub'=2] {'chan','sub'}, dimensions={0} | all-to-all | bytes 4718592 | tf_op jit(solution)/shard_map/all_to_all | solution.py:84
  380.1 40.7 %all_to_all.110 = bf16[128,96,96]{2,1,0:T(8,128)(2,1)S(1)} all-to-all(bf16[128,96,96]{2,1,0:T(8,128)(2,1)} %copy.32), channel_id=1, replica_groups=mesh['groups'=2,'dap'=4,'chan'=2,'sub'=2] {'chan','sub'}, dimensions={0} | all-to-all | bytes 4718592 | tf_op jit(solution)/shard_map/all_to_all | solution.py:83
  420.8 5.2 copy.41
  426.0 159.7 %all_to_all.111 = bf16[32,96,384]{1,0,2:T(8,128)(2,1)S(1)} all-to-all(bf16[32,96,384]{1,0,2:T(8,128)(2,1)} %bitcast.77), channel_id=1, replica_groups=mesh['groups'=2,'dap'=4,'chan'=2,'sub'=2] {'dap'}, dimensions={2} | all-to-all | bytes 4718592 | tf_op jit(solution)/shard_map/all_to_all | solution.py:86
  589.8 5.0 all_to_all.95
  594.7 13.0 %all-gather.2.cloned.1.call-done = bf16[32,384,384]{2,1,0:T(8,128)(2,1)} async-done(((bf16[32,96,384]{2,1,0:T(8,128)(2,1)}), bf16[32,384,384]{2,1,0:T(8,128)(2,1)}) %all-gather.2.cloned.1.call-update) | async-done | bytes 9437200 | tf_op jit(solution)/shard_map/all_gather | solution.py:90
  607.7 7.0 %convolution_convert_fusion = bf16[32,96,384]{2,1,0:T(8,128)(2,1)} fusion(bf16[32,384,96]{1,2,0:T(8,128)(2,1)S(1)} %all_to_all.95, bf16[32,384,384]{2,1,0:T(8,128)(2,1)} %all-gather.2.cloned.1.call-done), kind=kOutput, calls=%fused_computation.61 | convolution fusion | flops 907149312 | bytes 14155776 | tf_op jit(solution)/shard_map/cki,ckj->cij/dot_general | solution.py:87
  614.7 4.9 copy.39
  623.6 6.7 fusion.10
  630.3 30.2 %all-to-all-done.6 = bf16[32,96,384]{1,0,2:T(8,128)(2,1)S(1)} async-done(((bf16[32,96,384]{1,0,2:T(8,128)(2,1)}), bf16[32,96,384]{1,0,2:T(8,128)(2,1)S(1)}, u32[]{:S(2)}, u32[]{:S(2)}) %all-to-all-start.6) | async-done | bytes 2359328 | tf_op jit(solution)/shard_map/all_to_all | solution.py:93
  671.0 7.2 %reshape.154 = f32[128,9216]{1,0:T(8,128)} reshape(f32[4,32,96,96]{3,2,1,0:T(8,128)} %bitcast.71) | data formatting | bytes 9437184 | tf_op jit(solution)/shard_map/convert_element_type | solution.py:45
  678.1 8.0 %fusion.7 = bf16[9216,128]{1,0:T(8,128)(2,1)} fusion(f32[9216,128]{1,0:T(8,128)} %copy-done.4, f32[9216,128]{1,0:T(8,128)} %fusion.10, bf16[128,128]{1,0:T(8,128)(2,1)S(1)} %copy-done.10, f32[128,9216]{1,0:T(8,128)} %reshape.154, f32[128]{0:T(128)S(1)} %copy-done.14, f32[9216]{0:T(1024)S(1)} %rsqrt.47, f32[9216]{0:T(1024)S(1)} %div.63), kind=kOutput, calls=%fused_computation.13 | convolution fusion | flops 310247424 | bytes 16622080 | tf_op jit(solution)/shard_map/cx,cd->xd/dot_general | solution.py:47
  (85 shorter events, 112.6 us)
Async XLA Ops:
  6.5 13.7 %copy-start = (bf16[128,512]{1,0:T(8,128)(2,1)S(1)}, bf16[128,512]{1,0:T(8,128)(2,1)}, u32[]{:S(2)}) copy-start(bf16[128,512]{1,0:T(8,128)(2,1)} %param.13) | copy-start | bytes 393220
  6.5 7.3 %copy-start.5 = (bf16[96,96,128]{2,1,0:T(8,128)(2,1)S(1)}, bf16[96,96,128]{2,1,0:T(8,128)(2,1)}, u32[]{:S(2)}) copy-start(bf16[96,96,128]{2,1,0:T(8,128)(2,1)} %param.11) | copy-start | bytes 7077892
  6.5 7.3 %copy-start.13 = (f32[128]{0:T(128)S(1)}, f32[128]{0:T(128)}, u32[]{:S(2)}) copy-start(f32[128]{0:T(128)} %param.12) | copy-start | bytes 1540
  18.8 1.4 copy-start.7
  76.9 56.3 %collective-permute-start = (bf16[32,96,384]{2,1,0:T(8,128)(2,1)}, bf16[32,96,384]{2,1,0:T(8,128)(2,1)}, u32[]{:S(2)}, u32[]{:S(2)}) collective-permute-start(bf16[32,96,384]{2,1,0:T(8,128)(2,1)} %all_to_all.86), channel_id=1, source_target_pairs={{0,4},{4,8},{8,12},{12,0},{1,5},{5,9},{9,13},{13,1},{2,6},{6,10},{... | collective-permute-start | bytes 7077896 | tf_op jit(solution)/shard_map/ppermute | solution.py:17
  83.2 50.5 %all-to-all-start = ((bf16[128,96,96]{2,1,0:T(8,128)(2,1)}), bf16[128,96,96]{2,1,0:T(8,128)(2,1)S(1)}, u32[]{:S(2)}, u32[]{:S(2)}) async-start(bf16[128,96,96]{2,1,0:T(8,128)(2,1)} %copy.26), calls=%async_computation | async-start | bytes 6291456 | tf_op jit(solution)/shard_map/all_to_all | solution.py:67
  86.9 96.7 %collective-permute-start.2 = (bf16[32,96,384]{2,1,0:T(8,128)(2,1)}, bf16[32,96,384]{2,1,0:T(8,128)(2,1)}, u32[]{:S(2)}, u32[]{:S(2)}) collective-permute-start(bf16[32,96,384]{2,1,0:T(8,128)(2,1)} %all_to_all.86), channel_id=1, source_target_pairs={{0,12},{4,0},{8,4},{12,8},{1,13},{5,1},{9,5},{13,9},{2,14},{6,2},{... | collective-permute-start | bytes 7077896 | tf_op jit(solution)/shard_map/ppermute | solution.py:18
  133.2 99.7 %collective-permute-start.1 = (bf16[32,96,384]{2,1,0:T(8,128)(2,1)}, bf16[32,96,384]{2,1,0:T(8,128)(2,1)}, u32[]{:S(2)}, u32[]{:S(2)}) collective-permute-start(bf16[32,96,384]{2,1,0:T(8,128)(2,1)} %collective-permute-done), channel_id=1, source_target_pairs={{0,4},{4,8},{8,12},{12,0},{1,5},{5,9},{9,13},{13,1},{2,6},{6,10},{... | collective-permute-start | bytes 7077896 | tf_op jit(solution)/shard_map/ppermute | solution.py:17
  249.2 7.4 %copy-start.15 = (bf16[128,128]{1,0:T(8,128)(2,1)S(1)}, bf16[128,128]{1,0:T(8,128)(2,1)}, u32[]{:S(2)}) copy-start(bf16[128,128]{1,0:T(8,128)(2,1)} %param.14) | copy-start | bytes 98308
  252.6 40.6 %all-to-all-start.2 = ((bf16[32,96,384]{1,0,2:T(8,128)(2,1)}), bf16[32,96,384]{1,0,2:T(8,128)(2,1)S(1)}, u32[]{:S(2)}, u32[]{:S(2)}) async-start(bf16[32,96,384]{1,0,2:T(8,128)(2,1)} %copy.30), calls=%async_computation.2 | async-start | bytes 6291456 | tf_op jit(solution)/shard_map/all_to_all | solution.py:79
  256.3 351.4 %all-gather.2.cloned.1.call-start = ((), (), s32[]{:S(2)}) async-start(), calls=%async_computation.7 | async-start | bytes 11796480 | tf_op jit(solution)/shard_map/all_gather | solution.py:90
  298.0 4.6 copy-start.2
  303.7 7.4 %copy-start.6 = (bf16[96,96,128]{2,1,0:T(8,128)(2,1)S(1)}, bf16[96,96,128]{2,1,0:T(8,128)(2,1)}, u32[]{:S(2)}) copy-start(bf16[96,96,128]{2,1,0:T(8,128)(2,1)} %param.11) | copy-start | bytes 7077892
  303.7 7.4 %copy-start.9 = (bf16[128,128]{1,0:T(8,128)(2,1)S(1)}, bf16[128,128]{1,0:T(8,128)(2,1)}, u32[]{:S(2)}) copy-start(bf16[128,128]{1,0:T(8,128)(2,1)} %param.16) | copy-start | bytes 98308
  303.7 7.4 %copy-start.12 = (f32[128]{0:T(128)S(1)}, f32[128]{0:T(128)}, u32[]{:S(2)}) copy-start(f32[128]{0:T(128)} %param.15) | copy-start | bytes 1540
  317.1 5.5 copy-start.4
  317.1 2.8 copy-start.8
  317.1 2.8 copy-start.11
  614.7 8.9 %copy-start.16 = (bf16[128,128]{1,0:T(8,128)(2,1)S(1)}, bf16[128,128]{1,0:T(8,128)(2,1)}, u32[]{:S(2)}) copy-start(bf16[128,128]{1,0:T(8,128)(2,1)} %param.19) | copy-start | bytes 98308
  619.6 40.8 %all-to-all-start.6 = ((bf16[32,96,384]{1,0,2:T(8,128)(2,1)}), bf16[32,96,384]{1,0,2:T(8,128)(2,1)S(1)}, u32[]{:S(2)}, u32[]{:S(2)}) async-start(bf16[32,96,384]{1,0,2:T(8,128)(2,1)} %copy.39), calls=%async_computation.6 | async-start | bytes 6291456 | tf_op jit(solution)/shard_map/all_to_all | solution.py:93
  665.3 4.6 copy-start.3
  670.9 7.2 %copy-start.10 = (bf16[128,128]{1,0:T(8,128)(2,1)S(1)}, bf16[128,128]{1,0:T(8,128)(2,1)}, u32[]{:S(2)}) copy-start(bf16[128,128]{1,0:T(8,128)(2,1)} %param.21) | copy-start | bytes 98308
  671.0 7.2 %copy-start.14 = (f32[128]{0:T(128)S(1)}, f32[128]{0:T(128)}, u32[]{:S(2)}) copy-start(f32[128]{0:T(128)} %param.20) | copy-start | bytes 1540
  671.0 15.1 %copy-start.1 = (bf16[128,512]{1,0:T(8,128)(2,1)S(1)}, bf16[128,512]{1,0:T(8,128)(2,1)}, u32[]{:S(2)}) copy-start(bf16[128,512]{1,0:T(8,128)(2,1)} %param.13) | copy-start | bytes 393220
Sparse Core Ops, SparseCore 0:
  375.4 232.2 all-gather.1
